TPU v7x, 256 devices: a whole 4x4x8 slice. The times are simulated.
256 devices in a mesh: pix: 32 (over z, y), shell: 8 (over x, core).
Axes of the slice: x: 4, y: 4, z: 8, core: 2. Of those that a mesh axis runs over, the one named last changes fastest.
Arguments:
- field: float32 [128, 1048576], P('shell', 'pix'), may hold values from -3 to 3
- momentum: float32 [128, 1048576], P('shell', 'pix'), may hold values from -6 to 6
- kernels: float32 [4, 20, 128], P(None, None, 'shell'), may hold values from 0.002 to 0.02
- depth_class: int32 [1048576], P('pix'), may hold values from 0 to 3
- counts: int32 [20, 1048576], P(None, 'pix'), may hold values from 0 to 12
- mask: float32 [1048576], P('pix'), may hold values from 0.1 to 1.5, as said below
- mean_counts: float32 [20], replicated, may hold values from 1 to 8
- shell_scale: float32 [128], P('shell'), may hold values from 0.5 to 2
Outputs:
- gradient: float32 [128, 1048576], P('shell', 'pix')
- loglik: float32 [], replicated
Inputs may be any that keep to these rules, and one draw needn't show every extreme that they name: `mask`: mask weights are positive.
All inputs are finite; a program needn't handle non-finite values.
Results may differ from a plain program's by a relative error of at most 0.00005.
Values sent between devices are 32-bit elements; how exact they have to be, the bound alone decides.
No kernel may reach another device: no remote copies, remote signals or barrier semaphores. Data moves between devices by JAX's collectives and lax.ppermute only.
A program may use at most 128 MiB of HBM per device.

v0:
```python
import jax
import jax.numpy as jnp
from jax import lax
from jax.sharding import PartitionSpec as P

CYCLE = 2048
LEAP = 0.1
ANGULAR = 0.5
RADIAL = 0.5


def padded_2(cells, sides, width):
    for axis, dim in sides:
        count = lax.axis_size(axis)
        ends = count - 1
        head = lax.slice_in_dim(cells, 0, width, axis=dim)
        tail = lax.slice_in_dim(cells, cells.shape[dim] - width, cells.shape[dim], axis=dim)
        cells = jnp.concatenate(
            [
                lax.ppermute(tail, axis, [(i, (i + 1) % count) for i in range(ends)]),
                cells,
                lax.ppermute(head, axis, [((i + 1) % count, i) for i in range(ends)]),
            ],
            axis=dim,
        )
    return cells


def shards(field, momentum, kernels, depth_class, counts, mask, mean_counts, shell_scale):
    shells_here, pixels = field.shape
    classes, bins, _ = kernels.shape
    total_pix = pixels * lax.axis_size("pix")
    position = field + LEAP * momentum
    density = jnp.exp(position)
    flat = kernels.reshape(classes * bins, shells_here)
    onehot = (depth_class[None, :] == jnp.arange(classes, dtype=jnp.int32)[:, None]).astype(
        jnp.float32
    )
    every = jnp.dot(
        flat, density, precision=lax.Precision.HIGHEST, preferred_element_type=jnp.float32
    )
    partial_proj = jnp.sum(every.reshape(classes, bins, pixels) * onehot[:, None, :], axis=0)
    counted = counts.astype(jnp.float32)
    proj = lax.psum(partial_proj, "shell")
    weighted, total = lax.psum(
        (jnp.sum(mask[None, :] * proj, axis=1), jnp.sum(counted, axis=1)), "pix"
    )
    norm = weighted / total_pix
    rate = mean_counts[:, None] * mask[None, :] * proj / norm[:, None]
    local_sum = jnp.sum(counted * jnp.log(rate) - rate)
    loglik = lax.psum(local_sum, "pix") / (bins * total_pix)
    ratio = counted / proj - (total / (total_pix * norm))[:, None] * mask[None, :]
    padded = padded_2(position, (("pix", 1),), CYCLE)
    angular = (
        4.0 * position
        - padded[:, CYCLE - 1 : CYCLE - 1 + pixels]
        - padded[:, CYCLE + 1 : CYCLE + 1 + pixels]
    )
    angular = angular - padded[:, 0:pixels] - padded[:, 2 * CYCLE : 2 * CYCLE + pixels]
    stacked = padded_2(position, (("shell", 0),), 1)
    radial = 2.0 * position - stacked[:-2] - stacked[2:]
    spread = (onehot[:, None, :] * ratio[None, :, :]).reshape(classes * bins, pixels)
    back = lax.dot_general(
        flat,
        spread,
        (((0,), (0,)), ((), ())),
        precision=lax.Precision.HIGHEST,
        preferred_element_type=jnp.float32,
    )
    like = density * back
    gradient = (
        like
        - position / (shell_scale[:, None] * shell_scale[:, None])
        - ANGULAR * angular
        - RADIAL * radial
    )
    return (gradient, loglik)


def solution(mesh):
    placed = (
        P("shell", "pix"),
        P("shell", "pix"),
        P(None, None, "shell"),
        P("pix"),
        P(None, "pix"),
        P("pix"),
        P(),
        P("shell"),
    )
    return jax.shard_map(
        shards, mesh=mesh, in_specs=placed, out_specs=(P("shell", "pix"), P()), check_vma=False
    )
```

profile of v0, /device:TPU:8, one launch (start us, length us, event | category | flops | bytes accessed | tf_op | source)
XLA Modules:
  0.0 298.6 jit_solution(3591351216382486892)
XLA Ops:
  7.2 0.0 all-reduce.3.cloned.1.call-start
  7.2 0.8 copy.10
  8.0 0.1 reshape.36
  8.1 2.5 multiply_add_fusion
  10.5 0.0 copy-start.1
  10.5 10.9 %convolution_bitcast_fusion = f32[80,32768]{1,0:T(8,128)} fusion(f32[80,16]{0,1:T(8,128)S(1)} %reshape.36, f32[16,32768]{1,0:T(8,128)S(1)} %multiply_add_fusion), kind=kOutput, calls=%fused_computation | convolution fusion | flops 503316480 | bytes 12588032 | tf_op jit(solution)/shard_map/dot_general | solution.py:39
  21.4 0.0 copy-start.4
  21.4 11.4 %reshape.37 = f32[4,20,32768]{2,1,0:T(8,128)} reshape(f32[80,32768]{1,0:T(8,128)} %convolution_bitcast_fusion) | data formatting | bytes 20971520 | tf_op jit(solution)/shard_map/reshape | solution.py:42
  32.8 0.0 copy-done.4
  32.8 0.1 fusion.20
  32.9 0.0 copy-start.2
  32.9 0.8 copy-done.2
  33.7 8.0 %multiply_reduce_fusion = f32[20,32768]{1,0:T(8,128)} fusion(f32[4,20,32768]{2,1,0:T(8,128)} %reshape.37, f32[4,32768]{1,0:T(4,128)S(1)} %fusion.20), kind=kLoop, calls=%fused_computation.5 | loop fusion | flops 4587520 | bytes 13631488 | tf_op jit(solution)/shard_map/reduce_sum | solution.py:42
  41.7 0.0 copy-start.3
  41.7 0.0 all-reduce.3.cloned.1.call-update
  41.8 0.0 copy-start.6
  41.8 0.0 copy-start.5
  41.8 3.6 %collective-permute-start = (f32[16,2048]{1,0:T(8,128)S(1)}, f32[16,2048]{1,0:T(8,128)}, u32[]{:S(2)}, u32[]{:S(2)}) collective-permute-start(f32[16,2048]{1,0:T(8,128)S(1)} %get-tuple-element.8), channel_id=1, source_target_pairs={{0,8},{8,16},{16,24},{24,32},{32,40},{40,48},{48,56},{56,64},{64,7... | collective-permute-start | bytes 393224 | tf_op jit(solution)/shard_map/ppermute | solution.py:20
  45.4 3.0 %collective-permute-start.1 = (f32[16,2048]{1,0:T(8,128)S(1)}, f32[16,2048]{1,0:T(8,128)}, u32[]{:S(2)}, u32[]{:S(2)}) collective-permute-start(f32[16,2048]{1,0:T(8,128)S(1)} %get-tuple-element.9), channel_id=1, source_target_pairs={{8,0},{16,8},{24,16},{32,24},{40,32},{48,40},{56,48},{64,56},{72,6... | collective-permute-start | bytes 393224 | tf_op jit(solution)/shard_map/ppermute | solution.py:22
  48.4 0.0 copy-done.1
  48.5 0.9 fusion.21
  49.3 1.9 collective-permute-start.2
  51.3 1.3 collective-permute-start.3
  52.6 66.3 %all-reduce.3.cloned.1.call-done = f32[20,32768]{1,0:T(8,128)} async-done(((f32[20,32768]{1,0:T(8,128)}), f32[20,32768]{1,0:T(8,128)}) %all-reduce.3.cloned.1.call-update) | async-done | bytes 2621456 | tf_op jit(solution)/shard_map/psum | solution.py:44
  118.9 0.0 copy-done.3
  118.9 0.0 copy-start
  118.9 2.4 multiply_reduce_fusion.1
  121.3 0.0 copy-done.6
  121.3 71.1 %psum.30 = f32[20]{0:T(128)S(1)} all-reduce(f32[20]{0:T(128)S(1)} %multiply_reduce_fusion.1), channel_id=1, replica_groups=mesh['pix'=32,'shell'=8] {'pix'}, use_global_device_ids=true, to_apply=%region_5.0 | all-reduce | flops 20 | bytes 160 | tf_op jit(solution)/shard_map/psum | solution.py:45
  192.5 0.0 copy-done.5
  192.5 0.0 copy-done
  192.5 3.6 %subtract_reduce_fusion = (f32[]{:T(128)}, f32[20]{0:T(128)S(1)}) fusion(f32[20,32768]{1,0:T(8,128)S(1)} %copy-done, s32[20,32768]{1,0:T(8,128)} %param.12, f32[20]{0:T(128)S(1)} %broadcast_multiply_fusion, f32[20]{0:T(128)S(1)} %copy-done.5, f32[32768]{0:T(1024)S(1)} %copy-done.3), kind=kLoop, calls=%fused_computation.8 | loop fusion | flops 5242859 | bytes 5374196 | tf_op jit(solution)/shard_map/reduce_sum | solution.py:50
  196.1 74.9 %all-reduce = (f32[20]{0:T(128)S(1)}, f32[]{:T(128)}) all-reduce(f32[20]{0:T(128)S(1)} %get-tuple-element.3, f32[]{:T(128)} %get-tuple-element.2), channel_id=1, replica_groups=mesh['pix'=32,'shell'=8] {'pix'}, use_global_device_ids=true, to_apply=%region_3.0 | all-reduce | flops 21 | bytes 168 | tf_op jit(solution)/shard_map/psum | solution.py:45
  271.1 4.1 %multiply_subtract_fusion = f32[20,32768]{1,0:T(8,128)} fusion(f32[20,32768]{1,0:T(8,128)S(1)} %copy-done, s32[20,32768]{1,0:T(8,128)} %param.12, f32[20]{0:T(128)S(1)} %div.29, f32[32768]{0:T(1024)S(1)} %copy-done.3), kind=kLoop, calls=%fused_computation.9 | loop fusion | flops 2621440 | bytes 7995472 | tf_op jit(solution)/shard_map/sub | solution.py:52
  275.8 0.0 collective-permute-done
  275.8 0.0 collective-permute-done.1
  275.8 0.0 collective-permute-done.2
  275.8 0.0 collective-permute-done.3
  275.9 14.8 %fusion.11 = f32[16,32768]{1,0:T(8,128)} fusion(f32[16,32768]{1,0:T(8,128)} %copy-done.1, f32[16,2048]{1,0:T(8,128)} %collective-permute-done.1, f32[16,2048]{1,0:T(8,128)} %collective-permute-done, f32[1,32768]{1,0:T(1,128)} %collective-permute-done.3, f32[1,32768]{1,0:T(1,128)} %collective-permute-done.2, f32[4,20,16]{1,2,0:T(8,128)} %param.10, ...), kind=kOutput, calls=%fused_computation.22 | convolution fusion | flops 516947968 | bytes 7869504 | tf_op jit(solution)/shard_map/dot_general | solution.py:63
  (4 shorter events, 0.0 us)
Async XLA Ops:
  7.2 111.7 %all-reduce.3.cloned.1.call-start = ((), (), s32[]{:S(2)}) async-start(), calls=%async_computation | async-start | bytes 6291456 | tf_op jit(solution)/shard_map/psum | solution.py:44
  10.5 37.9 %copy-start.1 = (f32[16,32768]{1,0:T(8,128)}, f32[16,32768]{1,0:T(8,128)S(1)}, u32[]{:S(2)}) copy-start(f32[16,32768]{1,0:T(8,128)S(1)} %multiply_add_fusion) | copy-start | bytes 6291460
  21.4 11.4 %copy-start.4 = (s32[32768]{0:T(1024)S(1)}, s32[32768]{0:T(1024)}, u32[]{:S(2)}) copy-start(s32[32768]{0:T(1024)} %param.11) | copy-start | bytes 393220
  32.9 0.8 copy-start.2
  41.7 77.2 %copy-start.3 = (f32[32768]{0:T(1024)S(1)}, f32[32768]{0:T(1024)}, u32[]{:S(2)}) copy-start(f32[32768]{0:T(1024)} %param.13) | copy-start | bytes 393220
  41.8 79.6 %copy-start.6 = (f32[16]{0:T(128)S(1)}, f32[16]{0:T(128)}, u32[]{:S(2)}) copy-start(f32[16]{0:T(128)} %param.15) | copy-start | bytes 196
  41.8 150.7 %copy-start.5 = (f32[20]{0:T(128)S(1)}, f32[20]{0:T(128)}, u32[]{:S(2)}) copy-start(f32[20]{0:T(128)} %param.14) | copy-start | bytes 244
  41.8 234.0 %collective-permute-start = (f32[16,2048]{1,0:T(8,128)S(1)}, f32[16,2048]{1,0:T(8,128)}, u32[]{:S(2)}, u32[]{:S(2)}) collective-permute-start(f32[16,2048]{1,0:T(8,128)S(1)} %get-tuple-element.8), channel_id=1, source_target_pairs={{0,8},{8,16},{16,24},{24,32},{32,40},{40,48},{48,56},{56,64},{64,7... | collective-permute-start | bytes 393224 | tf_op jit(solution)/shard_map/ppermute | solution.py:20
  45.4 230.4 %collective-permute-start.1 = (f32[16,2048]{1,0:T(8,128)S(1)}, f32[16,2048]{1,0:T(8,128)}, u32[]{:S(2)}, u32[]{:S(2)}) collective-permute-start(f32[16,2048]{1,0:T(8,128)S(1)} %get-tuple-element.9), channel_id=1, source_target_pairs={{8,0},{16,8},{24,16},{32,24},{40,32},{48,40},{56,48},{64,56},{72,6... | collective-permute-start | bytes 393224 | tf_op jit(solution)/shard_map/ppermute | solution.py:22
  49.3 226.5 %collective-permute-start.2 = (f32[1,32768]{1,0:T(1,128)}, f32[1,32768]{1,0:T(1,128)}, u32[]{:S(2)}, u32[]{:S(2)}) collective-permute-start(f32[1,32768]{1,0:T(1,128)} %get-tuple-element.6), channel_id=1, source_target_pairs={{0,1},{1,2},{2,3},{3,4},{4,5},{5,6},{6,7},{8,9},{9,10},{10,11},{11... | collective-permute-start | bytes 393224 | tf_op jit(solution)/shard_map/ppermute | solution.py:20
  51.3 224.6 %collective-permute-start.3 = (f32[1,32768]{1,0:T(1,128)}, f32[1,32768]{1,0:T(1,128)}, u32[]{:S(2)}, u32[]{:S(2)}) collective-permute-start(f32[1,32768]{1,0:T(1,128)} %get-tuple-element.7), channel_id=1, source_target_pairs={{1,0},{2,1},{3,2},{4,3},{5,4},{6,5},{7,6},{9,8},{10,9},{11,10},{12... | collective-permute-start | bytes 393224 | tf_op jit(solution)/shard_map/ppermute | solution.py:22
  118.9 73.6 %copy-start = (f32[20,32768]{1,0:T(8,128)S(1)}, f32[20,32768]{1,0:T(8,128)}, u32[]{:S(2)}) copy-start(f32[20,32768]{1,0:T(8,128)} %all-reduce.3.cloned.1.call-done) | copy-start | bytes 7864324
Sparse Core Ops, SparseCore 0:
  41.9 76.9 all-reduce.2
where the time goes:
time: 299 us
  blocking collectives  146 us (49%)
  waiting for transfers between devices  66.4 us (22%)
  matrix products  25.7 us (9%)
  other arithmetic  20.8 us (7%)
  between operations  15.9 us (5%)
  local copies, waits for them, and re-layouts  14 us (5%)
  starting transfers between devices  9.87 us (3%)
    psum x2, blocking collectives, shards(): lax.psum((jnp.sum(mask[None, :] * proj, axis=1), jnp.sum(counted, axis=1)...  146 us
    psum x1, waiting for transfers between devices, shards(): proj = lax.psum(partial_proj, 'shell')  66.3 us
    dot_general x1, matrix products, shards(): lax.dot_general(flat, spread, (((0,), (0,)), ((), ())), precision=lax.Pre...  14.8 us
    reshape x1, local copies, waits for them, and re-layouts, shards(): every.reshape(classes, bins, pixels) * onehot[:, None, :]  11.4 us
    dot_general x1, matrix products, shards(): jnp.dot(flat, density, precision=lax.Precision.HIGHEST, preferred_element...  10.9 us
    reduce_sum x1, other arithmetic, shards(): jnp.sum(every.reshape(classes, bins, pixels) * onehot[:, None, :], axis=0)  8.02 us
  transfers between devices with their start and end apart: 5, of which 1 were waited for; matrix products, arithmetic and copies ran while one was open for 4% of the time, Pallas kernels for 0%

commit v1 on v0

--- a/solution.py
+++ b/solution.py
@@ -41,7 +41,9 @@
     )
     partial_proj = jnp.sum(every.reshape(classes, bins, pixels) * onehot[:, None, :], axis=0)
     counted = counts.astype(jnp.float32)
-    proj = lax.psum(partial_proj, "shell")
+    proj = partial_proj
+    for hop in (1, 2, 4):
+        proj = proj + lax.ppermute(proj, "shell", [(dev, dev ^ hop) for dev in range(8)])
     weighted, total = lax.psum(
         (jnp.sum(mask[None, :] * proj, axis=1), jnp.sum(counted, axis=1)), "pix"
     )

time: 299 us -> 359 us (1.20)
  waiting for transfers between devices: 66.4 us -> 131 us
  between operations: 15.9 us -> 2.54 us
  starting transfers between devices: 9.87 us -> 14.7 us
    ppermute x0 -> x3, waiting for transfers between devices: none -> 131 us  [shards(): lax.ppermute(proj, 'shell', [(dev, dev ^ hop) for dev in range(8)])]
    psum x1 -> x0, waiting for transfers between devices: 66.3 us -> none  [shards(): proj = lax.psum(partial_proj, 'shell')]
    ppermute x0 -> x3, starting transfers between devices: none -> 4.77 us  [shards(): lax.ppermute(proj, 'shell', [(dev, dev ^ hop) for dev in range(8)])]
  transfers between devices with their start and end apart: 5 -> 7, of which waited for: 1 -> 3; matrix products, arithmetic and copies ran while one was open for 4% -> 4% of each run, Pallas kernels for 0% -> 0%
where the time goes in v1:
time: 359 us
  blocking collectives  149 us (42%)
  waiting for transfers between devices  131 us (36%)
  matrix products  25.6 us (7%)
  other arithmetic  19.8 us (6%)
  local copies, waits for them, and re-layouts  16 us (4%)
  starting transfers between devices  14.7 us (4%)
    psum x2, blocking collectives, shards(): lax.psum((jnp.sum(mask[None, :] * proj, axis=1), jnp.sum(counted, axis=1)...  149 us
    ppermute x3, waiting for transfers between devices, shards(): lax.ppermute(proj, 'shell', [(dev, dev ^ hop) for dev in range(8)])  131 us
    dot_general x1, matrix products, shards(): lax.dot_general(flat, spread, (((0,), (0,)), ((), ())), precision=lax.Pre...  14.8 us
    reshape x1, local copies, waits for them, and re-layouts, shards(): every.reshape(classes, bins, pixels) * onehot[:, None, :]  11.4 us
    dot_general x1, matrix products, shards(): jnp.dot(flat, density, precision=lax.Precision.HIGHEST, preferred_element...  10.9 us
  transfers between devices with their start and end apart: 7, of which 3 were waited for; matrix products, arithmetic and copies ran while one was open for 4% of the time, Pallas kernels for 0%

profile of v1, /device:TPU:8, one launch (start us, length us, event | category | flops | bytes accessed | tf_op | source)
XLA Modules:
  0.0 358.6 jit_solution(10862470013400559715)
XLA Ops:
  0.6 0.8 copy.10
  1.4 0.1 reshape.36
  1.5 2.5 multiply_add_fusion
  3.9 0.0 copy-start.1
  4.0 10.9 %convolution_bitcast_fusion = f32[80,32768]{1,0:T(8,128)} fusion(f32[80,16]{0,1:T(8,128)S(1)} %reshape.36, f32[16,32768]{1,0:T(8,128)S(1)} %multiply_add_fusion), kind=kOutput, calls=%fused_computation | convolution fusion | flops 503316480 | bytes 12588032 | tf_op jit(solution)/shard_map/dot_general | solution.py:39
  14.8 0.0 copy-start.4
  14.8 11.4 %reshape.37 = f32[4,20,32768]{2,1,0:T(8,128)} reshape(f32[80,32768]{1,0:T(8,128)} %convolution_bitcast_fusion) | data formatting | bytes 20971520 | tf_op jit(solution)/shard_map/reshape | solution.py:42
  26.2 0.0 copy-done.4
  26.2 0.1 fusion.22
  26.4 0.0 copy-start.2
  26.4 6.2 %multiply_reduce_fusion = f32[20,32768]{1,0:T(8,128)S(1)} fusion(f32[4,20,32768]{2,1,0:T(8,128)} %reshape.37, f32[4,32768]{1,0:T(4,128)S(1)} %fusion.22), kind=kLoop, calls=%fused_computation.7 | loop fusion | flops 4587520 | bytes 13631488 | tf_op jit(solution)/shard_map/reduce_sum | solution.py:42
  32.6 0.0 copy-done.2
  32.6 0.1 collective-permute-start
  32.7 5.6 %collective-permute-done = f32[20,32768]{1,0:T(8,128)S(1)} collective-permute-done((f32[20,32768]{1,0:T(8,128)S(1)}, f32[20,32768]{1,0:T(8,128)S(1)}, u32[]{:S(2)}, u32[]{:S(2)}) %collective-permute-start) | collective-permute-done | bytes 2621472 | tf_op jit(solution)/shard_map/ppermute | solution.py:46
  38.4 0.4 add.19
  38.8 1.6 collective-permute-start.1
  40.4 0.0 copy-done.1
  40.4 3.5 collective-permute-start.3
  43.9 0.0 copy-start.3
  43.9 3.1 collective-permute-start.4
  47.0 62.0 %collective-permute-done.1 = f32[20,32768]{1,0:T(8,128)S(1)} collective-permute-done((f32[20,32768]{1,0:T(8,128)S(1)}, f32[20,32768]{1,0:T(8,128)S(1)}, u32[]{:S(2)}, u32[]{:S(2)}) %collective-permute-start.1) | collective-permute-done | bytes 2621472 | tf_op jit(solution)/shard_map/ppermute | solution.py:46
  109.0 0.3 add.20
  109.3 3.1 collective-permute-start.2
  112.4 2.4 fusion.23
  114.9 1.9 collective-permute-start.5
  116.8 0.0 copy-start.6
  116.8 0.0 copy-start.5
  116.8 1.4 collective-permute-start.6
  118.2 63.4 %collective-permute-done.2 = f32[20,32768]{1,0:T(8,128)S(1)} collective-permute-done((f32[20,32768]{1,0:T(8,128)S(1)}, f32[20,32768]{1,0:T(8,128)S(1)}, u32[]{:S(2)}, u32[]{:S(2)}) %collective-permute-start.2) | collective-permute-done | bytes 2621472 | tf_op jit(solution)/shard_map/ppermute | solution.py:46
  181.6 0.0 copy-done.3
  181.6 0.0 copy-start
  181.6 0.4 multiply_reduce_fusion.1
  182.1 1.2 copy-done
  183.3 0.0 copy-done.6
  183.3 73.8 %psum.22 = f32[20]{0:T(128)S(1)} all-reduce(f32[20]{0:T(128)S(1)} %multiply_reduce_fusion.1), channel_id=1, replica_groups=mesh['pix'=32,'shell'=8] {'pix'}, use_global_device_ids=true, to_apply=%region_4.0 | all-reduce | flops 20 | bytes 160 | tf_op jit(solution)/shard_map/psum | solution.py:47
  257.1 0.0 copy-done.5
  257.1 4.7 %subtract_reduce_fusion = (f32[]{:T(128)}, f32[20]{0:T(128)S(1)}) fusion(s32[20,32768]{1,0:T(8,128)} %param.12, f32[20]{0:T(128)S(1)} %broadcast_multiply_fusion, f32[20]{0:T(128)S(1)} %copy-done.5, f32[32768]{0:T(1024)S(1)} %copy-done.3, f32[20,32768]{1,0:T(8,128)S(1)} %add.20, f32[20,32768]{1,0:T(8,128)} %copy-done), kind=kLoop, calls=%fused_computation.10 | loop fusion | flops 5898219 | bytes 7995636 | tf_op jit(solution)/shard_map/reduce_sum | solution.py:52
  261.8 75.0 %all-reduce = (f32[20]{0:T(128)S(1)}, f32[]{:T(128)}) all-reduce(f32[20]{0:T(128)S(1)} %get-tuple-element.3, f32[]{:T(128)} %get-tuple-element.2), channel_id=1, replica_groups=mesh['pix'=32,'shell'=8] {'pix'}, use_global_device_ids=true, to_apply=%region_2.0 | all-reduce | flops 21 | bytes 168 | tf_op jit(solution)/shard_map/psum | solution.py:47
  336.8 5.1 %multiply_subtract_fusion = f32[20,32768]{1,0:T(8,128)} fusion(s32[20,32768]{1,0:T(8,128)} %param.12, f32[20]{0:T(128)S(1)} %div.29, f32[32768]{0:T(1024)S(1)} %copy-done.3, f32[20,32768]{1,0:T(8,128)S(1)} %add.20, f32[20,32768]{1,0:T(8,128)} %copy-done), kind=kLoop, calls=%fused_computation.11 | loop fusion | flops 3276800 | bytes 10616912 | tf_op jit(solution)/shard_map/sub | solution.py:54
  342.6 0.0 collective-permute-done.3
  342.6 0.0 collective-permute-done.4
  342.7 0.0 collective-permute-done.5
  342.7 0.0 collective-permute-done.6
  342.7 14.8 %fusion.6 = f32[16,32768]{1,0:T(8,128)} fusion(f32[4,20,16]{1,2,0:T(8,128)} %param.10, f32[20,32768]{1,0:T(8,128)} %multiply_subtract_fusion, f32[4,32768]{1,0:T(4,128)} %copy-done.2, f32[16,32768]{1,0:T(8,128)} %copy-done.1, f32[16,2048]{1,0:T(8,128)} %collective-permute-done.4, f32[16,2048]{1,0:T(8,128)} %collective-permute-done.3, ...), kind=kOutput, calls=%fused_computation.6 | convolution fusion | flops 516947968 | bytes 7869504 | tf_op jit(solution)/shard_map/dot_general | solution.py:65
  (4 shorter events, 0.0 us)
Async XLA Ops:
  3.9 36.4 %copy-start.1 = (f32[16,32768]{1,0:T(8,128)}, f32[16,32768]{1,0:T(8,128)S(1)}, u32[]{:S(2)}) copy-start(f32[16,32768]{1,0:T(8,128)S(1)} %multiply_add_fusion) | copy-start | bytes 6291460
  14.8 11.4 %copy-start.4 = (s32[32768]{0:T(1024)S(1)}, s32[32768]{0:T(1024)}, u32[]{:S(2)}) copy-start(s32[32768]{0:T(1024)} %param.11) | copy-start | bytes 393220
  26.4 6.3 %copy-start.2 = (f32[4,32768]{1,0:T(4,128)}, f32[4,32768]{1,0:T(4,128)S(1)}, u32[]{:S(2)}) copy-start(f32[4,32768]{1,0:T(4,128)S(1)} %fusion.22) | copy-start | bytes 1572868
  32.6 5.7 %collective-permute-start = (f32[20,32768]{1,0:T(8,128)S(1)}, f32[20,32768]{1,0:T(8,128)S(1)}, u32[]{:S(2)}, u32[]{:S(2)}) collective-permute-start(f32[20,32768]{1,0:T(8,128)S(1)} %multiply_reduce_fusion), channel_id=1, source_target_pairs={{0,1},{1,0},{2,3},{3,2},{4,5},{5,4},{6,7},{7,6},{8,9},{9,8},{10,11... | collective-permute-start | bytes 7864328 | tf_op jit(solution)/shard_map/ppermute | solution.py:46
  38.8 70.2 %collective-permute-start.1 = (f32[20,32768]{1,0:T(8,128)S(1)}, f32[20,32768]{1,0:T(8,128)S(1)}, u32[]{:S(2)}, u32[]{:S(2)}) collective-permute-start(f32[20,32768]{1,0:T(8,128)S(1)} %add.19), channel_id=1, source_target_pairs={{0,2},{1,3},{2,0},{3,1},{4,6},{5,7},{6,4},{7,5},{8,10},{9,11},{10,... | collective-permute-start | bytes 7864328 | tf_op jit(solution)/shard_map/ppermute | solution.py:46
  40.4 302.2 %collective-permute-start.3 = (f32[16,2048]{1,0:T(8,128)S(1)}, f32[16,2048]{1,0:T(8,128)}, u32[]{:S(2)}, u32[]{:S(2)}) collective-permute-start(f32[16,2048]{1,0:T(8,128)S(1)} %get-tuple-element.8), channel_id=1, source_target_pairs={{0,8},{8,16},{16,24},{24,32},{32,40},{40,48},{48,56},{56,64},{64,7... | collective-permute-start | bytes 393224 | tf_op jit(solution)/shard_map/ppermute | solution.py:20
  43.9 137.7 %copy-start.3 = (f32[32768]{0:T(1024)S(1)}, f32[32768]{0:T(1024)}, u32[]{:S(2)}) copy-start(f32[32768]{0:T(1024)} %param.13) | copy-start | bytes 393220
  43.9 298.8 %collective-permute-start.4 = (f32[16,2048]{1,0:T(8,128)S(1)}, f32[16,2048]{1,0:T(8,128)}, u32[]{:S(2)}, u32[]{:S(2)}) collective-permute-start(f32[16,2048]{1,0:T(8,128)S(1)} %get-tuple-element.9), channel_id=1, source_target_pairs={{8,0},{16,8},{24,16},{32,24},{40,32},{48,40},{56,48},{64,56},{72,6... | collective-permute-start | bytes 393224 | tf_op jit(solution)/shard_map/ppermute | solution.py:22
  109.3 72.3 %collective-permute-start.2 = (f32[20,32768]{1,0:T(8,128)S(1)}, f32[20,32768]{1,0:T(8,128)S(1)}, u32[]{:S(2)}, u32[]{:S(2)}) collective-permute-start(f32[20,32768]{1,0:T(8,128)S(1)} %add.20), channel_id=1, source_target_pairs={{0,4},{1,5},{2,6},{3,7},{4,0},{5,1},{6,2},{7,3},{8,12},{9,13},{10,... | collective-permute-start | bytes 7864328 | tf_op jit(solution)/shard_map/ppermute | solution.py:46
  114.9 227.8 %collective-permute-start.5 = (f32[1,32768]{1,0:T(1,128)}, f32[1,32768]{1,0:T(1,128)}, u32[]{:S(2)}, u32[]{:S(2)}) collective-permute-start(f32[1,32768]{1,0:T(1,128)} %get-tuple-element.6), channel_id=1, source_target_pairs={{0,1},{1,2},{2,3},{3,4},{4,5},{5,6},{6,7},{8,9},{9,10},{10,11},{11... | collective-permute-start | bytes 393224 | tf_op jit(solution)/shard_map/ppermute | solution.py:20
  116.8 66.5 %copy-start.6 = (f32[16]{0:T(128)S(1)}, f32[16]{0:T(128)}, u32[]{:S(2)}) copy-start(f32[16]{0:T(128)} %param.15) | copy-start | bytes 196
  116.8 140.3 %copy-start.5 = (f32[20]{0:T(128)S(1)}, f32[20]{0:T(128)}, u32[]{:S(2)}) copy-start(f32[20]{0:T(128)} %param.14) | copy-start | bytes 244
  116.8 225.9 %collective-permute-start.6 = (f32[1,32768]{1,0:T(1,128)}, f32[1,32768]{1,0:T(1,128)}, u32[]{:S(2)}, u32[]{:S(2)}) collective-permute-start(f32[1,32768]{1,0:T(1,128)} %get-tuple-element.7), channel_id=1, source_target_pairs={{1,0},{2,1},{3,2},{4,3},{5,4},{6,5},{7,6},{9,8},{10,9},{11,10},{12... | collective-permute-start | bytes 393224 | tf_op jit(solution)/shard_map/ppermute | solution.py:22
  181.6 1.7 copy-start
